TPU v7x, 128 devices: a whole 4x4x4 slice. The times are simulated.
128 devices in a mesh: dp: 4 (over x), seq: 16 (over y, z), mp: 2 (over core).
Axes of the slice: x: 4, y: 4, z: 4, core: 2. Of those that a mesh axis runs over, the one named last changes fastest.
Arguments:
- queries: bfloat16 [24576, 2048], P(('dp', 'seq'), 'mp'), may hold values from -64 to 64
- keys: bfloat16 [24576, 512], P(('dp', 'seq'), 'mp'), may hold values from -64 to 64
- values: bfloat16 [24576, 512], P(('dp', 'seq'), 'mp'), may hold values from -16 to 16
- offsets: int32 [24576], P(('dp', 'seq')), may hold values from 0 to 6143, as said below
- out_weight: bfloat16 [2048, 4096], P('mp'), may hold values from -0.125 to 0.125
- stream_in: bfloat16 [24576, 4096], P(('dp', 'seq'), 'mp'), may hold values from -64 to 64
- norm_gain: float32 [4096], replicated, may hold values from 0.1 to 1.9
- head_weight: bfloat16 [65536, 4096], P(('dp', 'seq', 'mp')), may hold values from -15 to 15
- picks: int32 [1024], P(('dp', 'seq')), may hold values from 0 to 383
- targets: int32 [1024], replicated, may hold values from 0 to 65535
Outputs:
- stream_out: bfloat16 [24576, 4096], P(('dp', 'seq'), 'mp')
- logprob: float32 [1024], P(('dp', 'seq', 'mp'))
Inputs may be any that keep to these rules, and one draw needn't show every extreme that they name: Each pack is cut into two to four consecutive rollouts; offsets[t] is the first position of the rollout that holds t, so offsets[t] <= t % 6144, and t % 6144 - offsets[t] is at most 3071, reached in every pack.
All inputs are finite; a program needn't handle non-finite values.
Results may differ from a plain program's by a relative error of at most 0.013.
Values may be sent and summed in bfloat16 or wider, within the bound.
No kernel may reach another device: no remote copies, remote signals or barrier semaphores. Data moves between devices by JAX's collectives and lax.ppermute only.
A program may use at most 128 MiB of HBM per device.

v0:
```python
import math
import jax
import jax.numpy as jnp
from jax import lax
from jax.sharding import PartitionSpec as P

HD = 128
GROUP = 4


def rounded_term(left, right):
    term = jnp.dot(left, right, preferred_element_type=jnp.float32)
    term = lax.optimization_barrier(term.astype(jnp.bfloat16))
    return term.astype(jnp.float32)


def on_device(
    queries, keys, values, offsets, out_weight, stream_in, norm_gain, head_weight, picks, targets
):
    rows_dev = queries.shape[0]
    block_rows = min(512, rows_dev)
    heads_dev = queries.shape[1] // HD
    groups_dev = keys.shape[1] // HD
    scale = 1.0 / math.sqrt(HD)
    seq_count = lax.axis_size("seq")
    reach_len = rows_dev * seq_count // 2
    pack_base = lax.axis_index("seq") * rows_dev
    stacked = jnp.stack([keys, values])
    whole = lax.all_gather(stacked, "seq", axis=1, tiled=True)
    padded = jnp.pad(whole, ((0, 0), (reach_len, 0), (0, 0)))
    joined = lax.dynamic_slice(
        padded, (0, pack_base, 0), (2, reach_len + rows_dev, stacked.shape[2])
    )
    window = reach_len + block_rows
    block_count = rows_dev // block_rows

    def attend(item):
        block = item // groups_dev
        group = item % groups_dev
        first = block * block_rows
        q_part = lax.dynamic_slice(queries, (first, group * GROUP * HD), (block_rows, GROUP * HD))
        q_part = q_part.reshape(block_rows, GROUP, HD)
        kv_part = lax.dynamic_slice(joined, (0, first, group * HD), (2, window, HD))
        scores = (
            jnp.einsum("qha,ka->hqk", q_part, kv_part[0], preferred_element_type=jnp.float32)
            * scale
        )
        query_pos = pack_base + first + jnp.arange(block_rows, dtype=jnp.int32)
        key_pos = pack_base - reach_len + first + jnp.arange(window, dtype=jnp.int32)
        allowed = (key_pos[None, :] >= offsets[:, None]) & (key_pos[None, :] <= query_pos[:, None])
        scores = jnp.where(allowed[None], scores, -jnp.inf)
        top = jnp.max(scores, axis=-1, keepdims=True)
        weights = jnp.exp(scores - top)
        probs = (weights / jnp.sum(weights, axis=-1, keepdims=True)).astype(jnp.bfloat16)
        mixed = jnp.einsum("hqk,ka->qha", probs, kv_part[1], preferred_element_type=jnp.float32)
        return mixed.astype(jnp.bfloat16).reshape(block_rows, GROUP * HD)

    pieces = lax.map(attend, jnp.arange(block_count * groups_dev, dtype=jnp.int32))
    context = pieces.reshape(block_count, groups_dev, block_rows, GROUP * HD).transpose(0, 2, 1, 3)
    context = context.reshape(rows_dev, heads_dev * HD)
    partial_terms = rounded_term(context, out_weight)
    branch = lax.psum_scatter(
        partial_terms.astype(jnp.bfloat16), "mp", scatter_dimension=1, tiled=True
    ).astype(jnp.float32)
    stream_out = (stream_in.astype(jnp.float32) + branch).astype(jnp.bfloat16)
    chosen = jnp.take(stream_out, picks, axis=0)
    full_rows = lax.all_gather(chosen, "mp", axis=1, tiled=True).astype(jnp.float32)
    inverse = lax.rsqrt(jnp.mean(full_rows * full_rows, axis=-1, keepdims=True) + 1e-05)
    normed = (full_rows * inverse * norm_gain).astype(jnp.bfloat16)
    logits = lax.dot_general(
        lax.all_gather(normed, ("dp", "seq"), axis=0, tiled=True),
        head_weight,
        (((1,), (1,)), ((), ())),
        preferred_element_type=jnp.float32,
    )
    vocab_rows = head_weight.shape[0]
    flat_index = lax.axis_index(("dp", "seq", "mp"))
    vocab_first = flat_index * vocab_rows
    hit = targets[:, None] == vocab_first + jnp.arange(vocab_rows, dtype=jnp.int32)[None, :]
    target_part = jnp.sum(jnp.where(hit, logits, 0.0), axis=-1)
    local_top = jnp.max(logits, axis=-1)
    out_rows = logits.shape[0] // lax.axis_size(("dp", "seq", "mp"))
    own_first = flat_index * out_rows
    top_all = lax.pmax(local_top, ("dp", "seq", "mp"))
    expsum = jnp.sum(jnp.exp(logits - top_all[:, None]), axis=-1)
    total, target_logit = (
        lax.psum_scatter(expsum, ("dp", "seq", "mp"), scatter_dimension=0, tiled=True),
        lax.psum_scatter(target_part, ("dp", "seq", "mp"), scatter_dimension=0, tiled=True),
    )
    top_own = lax.dynamic_slice_in_dim(top_all, own_first, out_rows)
    logprob = target_logit - top_own - jnp.log(total)
    return (stream_out, logprob)


def solution(mesh):
    placed = (
        P(("dp", "seq"), "mp"),
        P(("dp", "seq"), "mp"),
        P(("dp", "seq"), "mp"),
        P(("dp", "seq")),
        P("mp", None),
        P(("dp", "seq"), "mp"),
        P(),
        P(("dp", "seq", "mp"), None),
        P(("dp", "seq")),
        P(),
    )
    return jax.shard_map(
        on_device,
        mesh=mesh,
        in_specs=placed,
        out_specs=(P(("dp", "seq"), "mp"), P(("dp", "seq", "mp"))),
        check_vma=False,
    )
```

profile of v0, /device:TPU:1, one launch (start us, length us, event | category | flops | bytes accessed | tf_op | source)
XLA Modules:
  0.0 392.5 jit_solution(1795394309466374496)
XLA Ops:
  7.2 1.8 pad_maximum_fusion
  9.2 65.4 %all-gather.3.cloned.1.call-done = bf16[2,6144,256]{2,1,0:T(8,128)(2,1)} async-done(((bf16[2,384,256]{2,1,0:T(8,128)(2,1)}), bf16[2,6144,256]{2,1,0:T(8,128)(2,1)}) %all-gather.3.cloned.1.call-update) | async-done | bytes 6291472 | tf_op jit(solution)/shard_map/all_gather | solution.py:29
  74.6 3.6 pad_dynamic-slice_fusion
  78.2 56.9 %while.12 = (s32[]{:T(128)}, bf16[2,384,512]{1,2,0:T(8,128)(2,1)}, s32[2]{0:T(128)S(1)}, bf16[2,3456,256]{2,1,0:T(8,128)(2,1)}, s32[]{:T(128)}, /*index=5*/s32[3...) while((s32[]{:T(128)}, bf16[2,384,512]{1,2,0:T(8,128)(2,1)}, ...), condition=%wide.region_3.4_spmd, body=%wide.region_0.3_spmd.sunk | while | flops 2753944576 | bytes 56373324 | solution.py:58
  78.2 0.7 dynamic_slice.35
  81.7 1.7 compare_and_fusion.3
  83.7 13.0 %fusion.33 = (f32[4,384]{1,0:T(4,128)S(1)}, f32[4,384,3456]{1,2,0:T(8,128)}) fusion(pred[384,3456]{0,1:T(8,128)(4,1)S(1)} %compare_and_fusion.3, bf16[384,4,128]{0,2,1:T(8,128)(2,1)S(1)} %bitcast.61, bf16[2,3456,256]{2,1,0:T(8,128)(2,1)} %get-tuple-element.235, s32[]{:T(128)S(6)} %select_n.88), kind=kOutput, calls=%fused_computation.45.clone.1 | convolution fusion | flops 1380191616 | bytes 23844868 | tf_op jit(solution)/shard_map/while/body/eval_jaxpr/sub | solution.py:53
  96.7 9.0 %fusion.34 = bf16[128,4,384]{2,0,1:T(8,128)(2,1)S(1)} fusion(f32[4,384,3456]{1,2,0:T(8,128)} %get-tuple-element.194, f32[4,384]{1,0:T(4,128)S(1)} %get-tuple-element.195, bf16[2,3456,256]{2,1,0:T(8,128)(2,1)} %get-tuple-element.235, s32[]{:T(128)S(6)} %add.164, s32[]{:T(128)S(6)} %select_n.88), kind=kOutput, calls=%fused_computation.12.clone.1 | convolution fusion | flops 1369767936 | bytes 22517768 | tf_op jit(solution)/shard_map/while/body/eval_jaxpr/hqk,ka->qha/dot_general | solution.py:55
  105.8 0.9 copy-done.7
  106.7 0.7 dynamic_slice.35
  110.1 1.7 compare_and_fusion.3
  112.1 13.0 %fusion.33 = (f32[4,384]{1,0:T(4,128)S(1)}, f32[4,384,3456]{1,2,0:T(8,128)}) fusion(pred[384,3456]{0,1:T(8,128)(4,1)S(1)} %compare_and_fusion.3, bf16[384,4,128]{0,2,1:T(8,128)(2,1)S(1)} %bitcast.61, bf16[2,3456,256]{2,1,0:T(8,128)(2,1)} %get-tuple-element.235, s32[]{:T(128)S(6)} %select_n.88), kind=kOutput, calls=%fused_computation.45.clone.1 | convolution fusion | flops 1380191616 | bytes 23844868 | tf_op jit(solution)/shard_map/while/body/eval_jaxpr/sub | solution.py:53
  125.1 9.0 %fusion.34 = bf16[128,4,384]{2,0,1:T(8,128)(2,1)S(1)} fusion(f32[4,384,3456]{1,2,0:T(8,128)} %get-tuple-element.194, f32[4,384]{1,0:T(4,128)S(1)} %get-tuple-element.195, bf16[2,3456,256]{2,1,0:T(8,128)(2,1)} %get-tuple-element.235, s32[]{:T(128)S(6)} %add.164, s32[]{:T(128)S(6)} %select_n.88), kind=kOutput, calls=%fused_computation.12.clone.1 | convolution fusion | flops 1369767936 | bytes 22517768 | tf_op jit(solution)/shard_map/while/body/eval_jaxpr/hqk,ka->qha/dot_general | solution.py:55
  134.3 0.9 copy-done.7
  135.1 8.8 %convolution_convert_fusion = bf16[384,4096]{1,0:T(8,128)(2,1)} fusion(bf16[384,1024]{0,1:T(8,128)(2,1)} %bitcast.65, bf16[1024,4096]{1,0:T(8,128)(2,1)} %param.16), kind=kOutput, calls=%fused_computation.26 | convolution fusion | flops 3222798336 | bytes 12320768 | tf_op jit(solution)/shard_map/dot_general | solution.py:12
  144.2 14.6 %reduce-scatter.2.cloned.1.call-done = bf16[384,2048]{1,0:T(8,128)(2,1)} async-done(((bf16[384,4096]{1,0:T(8,128)(2,1)}), bf16[384,2048]{1,0:T(8,128)(2,1)}) %reduce-scatter.2.cloned.1.call-update) | async-done | bytes 1572880 | tf_op jit(solution)/shard_map/reduce_scatter | solution.py:62
  158.8 2.0 add_convert_fusion
  161.6 2.0 all_gather.10
  163.7 0.8 fusion.19
  164.5 79.4 %all-gather.5.cloned.1.call-done = bf16[1024,4096]{1,0:T(8,128)(2,1)} async-done(((bf16[16,4096]{1,0:T(8,128)(2,1)}), bf16[1024,4096]{1,0:T(8,128)(2,1)}) %all-gather.5.cloned.1.call-update) | async-done | bytes 8388624 | tf_op jit(solution)/shard_map/all_gather | solution.py:71
  243.9 10.5 %fusion.22 = (f32[1024]{0:T(1024)S(1)}, f32[1024,512]{0,1:T(8,128)}) fusion(bf16[1024,4096]{1,0:T(8,128)(2,1)} %all-gather.5.cloned.1.call-done, bf16[512,4096]{1,0:T(8,128)(2,1)} %param.19), kind=kOutput, calls=%fused_computation.46 | convolution fusion | flops 4295490560 | bytes 14684160 | tf_op jit(solution)/shard_map/dot_general | solution.py:70
  254.4 64.7 %pmax.7 = f32[1024]{0:T(1024)S(1)} all-reduce(f32[1024]{0:T(1024)S(1)} %get-tuple-element.141), channel_id=1, replica_groups=mesh['dp'=4,'seq'=16,'mp'=2] {'dp','seq','mp'}, use_global_device_ids=true, to_apply=%region_9.10 | all-reduce | flops 1024 | bytes 8192 | tf_op jit(solution)/shard_map/pmax | solution.py:84
  319.1 2.1 select_reduce_fusion
  321.1 64.3 %all-reduce.3 = (f32[1024]{0:T(1024)S(1)}, f32[1024]{0:T(1024)S(1)}) all-reduce(f32[1024]{0:T(1024)S(1)} %get-tuple-element.120, f32[1024]{0:T(1024)S(1)} %get-tuple-element.119), channel_id=4, replica_groups=mesh['dp'=4,'seq'=16,'mp'=2] {'dp','seq','mp'}, use_global_device_ids=true, to_apply=%region_11.12.clone | all-reduce | flops 2048 | bytes 16384
  (47 shorter events, 2.5 us)
Async XLA Ops:
  7.2 67.4 %all-gather.3.cloned.1.call-start = ((), (), s32[]{:S(2)}) async-start(), calls=%async_computation.1 | async-start | bytes 6684672 | tf_op jit(solution)/shard_map/all_gather | solution.py:29
  9.1 149.8 %reduce-scatter.2.cloned.1.call-start = ((), (), s32[]{:S(2)}) async-start(), calls=%async_computation.2 | async-start | bytes 4718592 | tf_op jit(solution)/shard_map/reduce_scatter | solution.py:62
  9.1 69.1 %copy-start = (bf16[384,1024]{1,0:T(8,128)(2,1)S(1)}, bf16[384,1024]{1,0:T(8,128)(2,1)}, u32[]{:S(2)}) copy-start(bf16[384,1024]{1,0:T(8,128)(2,1)} %param.12) | copy-start | bytes 2359300
  9.1 69.1 %copy-start.3 = (s32[384]{0:T(512)S(1)}, s32[384]{0:T(512)}, u32[]{:S(2)}) copy-start(s32[384]{0:T(512)} %param.15) | copy-start | bytes 4612
  96.7 9.0 %copy-start.6 = (bf16[2,384,512]{1,2,0:T(8,128)(2,1)S(1)}, bf16[2,384,512]{1,2,0:T(8,128)(2,1)}, u32[]{:S(2)}) copy-start(bf16[2,384,512]{1,2,0:T(8,128)(2,1)} %get-tuple-element.215) | copy-start | bytes 2359300 | tf_op jit(solution)/shard_map/while
  105.8 0.9 copy-start.7
  125.1 9.0 %copy-start.6 = (bf16[2,384,512]{1,2,0:T(8,128)(2,1)S(1)}, bf16[2,384,512]{1,2,0:T(8,128)(2,1)}, u32[]{:S(2)}) copy-start(bf16[2,384,512]{1,2,0:T(8,128)(2,1)} %get-tuple-element.215) | copy-start | bytes 2359300 | tf_op jit(solution)/shard_map/while
  134.2 0.9 copy-start.7
  135.1 9.1 %copy-start.8 = (s32[16]{0:T(128)S(1)}, s32[16]{0:T(128)}, u32[]{:S(2)}) copy-start(s32[16]{0:T(128)} %param.20) | copy-start | bytes 196
  143.9 14.9 %copy-start.2 = (bf16[384,2048]{1,0:T(8,128)(2,1)S(1)}, bf16[384,2048]{1,0:T(8,128)(2,1)}, u32[]{:S(2)}) copy-start(bf16[384,2048]{1,0:T(8,128)(2,1)} %param.17) | copy-start | bytes 4718596
  143.9 19.8 %copy-start.4 = (f32[4096]{0:T(1024)S(1)}, f32[4096]{0:T(1024)}, u32[]{:S(2)}) copy-start(f32[4096]{0:T(1024)} %param.18) | copy-start | bytes 49156
  143.9 99.9 %all-gather.5.cloned.1.call-start = ((), (), s32[]{:S(2)}) async-start(), calls=%async_computation.3 | async-start | bytes 8519680 | tf_op jit(solution)/shard_map/all_gather | solution.py:71
  160.9 93.5 %copy-start.1 = (bf16[384,2048]{1,0:T(8,128)(2,1)}, bf16[384,2048]{1,0:T(8,128)(2,1)S(1)}, u32[]{:S(2)}) copy-start(bf16[384,2048]{1,0:T(8,128)(2,1)S(1)} %add_convert_fusion) | copy-start | bytes 4718596
  164.5 154.5 %copy-start.5 = (s32[1024]{0:T(1024)S(1)}, s32[1024]{0:T(1024)}, u32[]{:S(2)}) copy-start(s32[1024]{0:T(1024)} %param.21) | copy-start | bytes 12292
Sparse Core Ops, SparseCore 0:
  10.1 64.4 all-gather.2
  144.1 14.7 reduce-scatter.1
  164.6 79.2 all-gather.4
where the time goes:
time: 393 us
  waiting for transfers between devices  159 us (40%)
  blocking collectives  131 us (33%)
  matrix products  63.3 us (16%)
  between operations  13.9 us (4%)
  other arithmetic  10.9 us (3%)
  local copies, waits for them, and re-layouts  7.97 us (2%)
  loops' own time  5.79 us (1%)
    all_gather x1, waiting for transfers between devices, on_device(): lax.all_gather(normed, ('dp', 'seq'), axis=0, tiled=True)  79.4 us
    all_gather x1, waiting for transfers between devices, on_device(): whole = lax.all_gather(stacked, 'seq', axis=1, tiled=True)  65.4 us
    pmax x1, blocking collectives, on_device(): top_all = lax.pmax(local_top, ('dp', 'seq', 'mp'))  64.7 us
    unnamed x1, blocking collectives  64.3 us
    sub x2, matrix products, attend(): weights = jnp.exp(scores - top)  26.1 us
    dot_general x2, matrix products, attend(): jnp.einsum('hqk,ka->qha', probs, kv_part[1], preferred_element_type=jnp.f...  18 us
    reduce_scatter x1, waiting for transfers between devices, on_device(): lax.psum_scatter(partial_terms.astype(jnp.bfloat16), 'mp', scatter_dimens...  14.6 us
    dot_general x1, matrix products, on_device(): lax.dot_general(lax.all_gather(normed, ('dp', 'seq'), axis=0, tiled=True)...  10.5 us
  transfers between devices with their start and end apart: 3, of which 3 were waited for; matrix products, arithmetic and copies ran while one was open for 0% of the time, Pallas kernels for 0%

commit v1 on v0

--- a/solution.py
+++ b/solution.py
@@ -26,7 +26,9 @@
     reach_len = rows_dev * seq_count // 2
     pack_base = lax.axis_index("seq") * rows_dev
     stacked = jnp.stack([keys, values])
-    whole = lax.all_gather(stacked, "seq", axis=1, tiled=True)
+    whole = jnp.concatenate(
+        lax.all_to_all(jnp.stack([stacked] * lax.axis_size("seq")), "seq", 0, 0), axis=1
+    )
     padded = jnp.pad(whole, ((0, 0), (reach_len, 0), (0, 0)))
     joined = lax.dynamic_slice(
         padded, (0, pack_base, 0), (2, reach_len + rows_dev, stacked.shape[2])

time: 393 us -> 450 us (1.15)
  waiting for transfers between devices: 159 us -> 201 us
  starting transfers between devices: 0.3 us -> 8.71 us
  local copies, waits for them, and re-layouts: 7.97 us -> 15.1 us
    all_to_all x0 -> x1, waiting for transfers between devices: none -> 98.5 us  [on_device(): lax.all_to_all(jnp.stack([stacked] * lax.axis_size('seq')), 'seq', 0, 0)]
    all_gather x1 -> x0, waiting for transfers between devices: 65.4 us -> none  [on_device(): whole = lax.all_gather(stacked, 'seq', axis=1, tiled=True)]
    all_to_all x0 -> x1, starting transfers between devices: none -> 8.63 us  [on_device(): lax.all_to_all(jnp.stack([stacked] * lax.axis_size('seq')), 'seq', 0, 0)]
    reduce_scatter x1, waiting for transfers between devices: 14.6 us -> 23.1 us  [on_device(): lax.psum_scatter(partial_terms.astype(jnp.bfloat16), 'mp', scatter_dimens...]
where the time goes in v1:
time: 450 us; the launch traced here: 449 us
  waiting for transfers between devices  201 us (45%)
  blocking collectives  131 us (29%)
  matrix products  63.3 us (14%)
  local copies, waits for them, and re-layouts  15.1 us (3%)
  between operations  14.2 us (3%)
  other arithmetic  10.1 us (2%)
  starting transfers between devices  8.71 us (2%)
  loops' own time  5.79 us (1%)
    all_to_all x1, waiting for transfers between devices, on_device(): lax.all_to_all(jnp.stack([stacked] * lax.axis_size('seq')), 'seq', 0, 0)  98.5 us
    all_gather x1, waiting for transfers between devices, on_device(): lax.all_gather(normed, ('dp', 'seq'), axis=0, tiled=True)  79.4 us
    pmax x1, blocking collectives, on_device(): top_all = lax.pmax(local_top, ('dp', 'seq', 'mp'))  64.7 us
    unnamed x1, blocking collectives  64.3 us
    sub x2, matrix products, attend(): weights = jnp.exp(scores - top)  26.1 us
    reduce_scatter x1, waiting for transfers between devices, on_device(): lax.psum_scatter(partial_terms.astype(jnp.bfloat16), 'mp', scatter_dimens...  23.1 us
    dot_general x2, matrix products, attend(): jnp.einsum('hqk,ka->qha', probs, kv_part[1], preferred_element_type=jnp.f...  18 us
    dot_general x1, matrix products, on_device(): lax.dot_general(lax.all_gather(normed, ('dp', 'seq'), axis=0, tiled=True)...  10.5 us
  transfers between devices with their start and end apart: 3, of which 3 were waited for; matrix products, arithmetic and copies ran while one was open for 0% of the time, Pallas kernels for 0%

profile of v1, /device:TPU:1, one launch (start us, length us, event | category | flops | bytes accessed | tf_op | source)
XLA Modules:
  0.0 449.3 jit_solution(3709787078647884581)
XLA Ops:
  7.2 1.1 pad_maximum_fusion
  8.2 3.4 stack.11
  11.6 8.6 %all-to-all-start = ((bf16[16,2,384,256]{3,2,1,0:T(8,128)(2,1)}), bf16[16,2,384,256]{3,2,1,0:T(8,128)(2,1)}, u32[]{:S(2)}, u32[]{:S(2)}) async-start(bf16[16,2,384,256]{3,2,1,0:T(8,128)(2,1)} %stack.11), calls=%async_computation | async-start | bytes 12582912 | tf_op jit(solution)/shard_map/all_to_all | solution.py:30
  20.3 98.5 %all-to-all-done = bf16[16,2,384,256]{3,2,1,0:T(8,128)(2,1)} async-done(((bf16[16,2,384,256]{3,2,1,0:T(8,128)(2,1)}), bf16[16,2,384,256]{3,2,1,0:T(8,128)(2,1)}, u32[]{:S(2)}, u32[]{:S(2)}) %all-to-all-start) | async-done | bytes 6291488 | tf_op jit(solution)/shard_map/all_to_all | solution.py:30
  118.8 3.2 copy.25
  122.1 4.2 pad_dynamic-slice_fusion
  126.2 56.9 %while.12 = (s32[]{:T(128)}, bf16[2,384,512]{1,2,0:T(8,128)(2,1)}, s32[2]{0:T(128)S(1)}, bf16[2,3456,256]{2,1,0:T(8,128)(2,1)}, s32[]{:T(128)}, /*index=5*/s32[3...) while((s32[]{:T(128)}, bf16[2,384,512]{1,2,0:T(8,128)(2,1)}, ...), condition=%wide.region_3.4_spmd, body=%wide.region_0.3_spmd.sunk | while | flops 2753944576 | bytes 56373324 | solution.py:60
  129.7 1.7 compare_and_fusion.3
  131.7 13.0 %fusion.33 = (f32[4,384]{1,0:T(4,128)S(1)}, f32[4,384,3456]{1,2,0:T(8,128)}) fusion(pred[384,3456]{0,1:T(8,128)(4,1)S(1)} %compare_and_fusion.3, bf16[384,4,128]{0,2,1:T(8,128)(2,1)S(1)} %bitcast.65, bf16[2,3456,256]{2,1,0:T(8,128)(2,1)} %get-tuple-element.243, s32[]{:T(128)S(6)} %select_n.88), kind=kOutput, calls=%fused_computation.45.clone.1 | convolution fusion | flops 1380191616 | bytes 23844868 | tf_op jit(solution)/shard_map/while/body/eval_jaxpr/sub | solution.py:55
  144.7 9.0 %fusion.34 = bf16[128,4,384]{2,0,1:T(8,128)(2,1)S(1)} fusion(f32[4,384,3456]{1,2,0:T(8,128)} %get-tuple-element.202, f32[4,384]{1,0:T(4,128)S(1)} %get-tuple-element.203, bf16[2,3456,256]{2,1,0:T(8,128)(2,1)} %get-tuple-element.243, s32[]{:T(128)S(6)} %add.164, s32[]{:T(128)S(6)} %select_n.88), kind=kOutput, calls=%fused_computation.12.clone.1 | convolution fusion | flops 1369767936 | bytes 22517768 | tf_op jit(solution)/shard_map/while/body/eval_jaxpr/hqk,ka->qha/dot_general | solution.py:57
  153.8 0.9 copy-done.7
  158.2 1.7 compare_and_fusion.3
  160.2 13.0 %fusion.33 = (f32[4,384]{1,0:T(4,128)S(1)}, f32[4,384,3456]{1,2,0:T(8,128)}) fusion(pred[384,3456]{0,1:T(8,128)(4,1)S(1)} %compare_and_fusion.3, bf16[384,4,128]{0,2,1:T(8,128)(2,1)S(1)} %bitcast.65, bf16[2,3456,256]{2,1,0:T(8,128)(2,1)} %get-tuple-element.243, s32[]{:T(128)S(6)} %select_n.88), kind=kOutput, calls=%fused_computation.45.clone.1 | convolution fusion | flops 1380191616 | bytes 23844868 | tf_op jit(solution)/shard_map/while/body/eval_jaxpr/sub | solution.py:55
  173.2 9.0 %fusion.34 = bf16[128,4,384]{2,0,1:T(8,128)(2,1)S(1)} fusion(f32[4,384,3456]{1,2,0:T(8,128)} %get-tuple-element.202, f32[4,384]{1,0:T(4,128)S(1)} %get-tuple-element.203, bf16[2,3456,256]{2,1,0:T(8,128)(2,1)} %get-tuple-element.243, s32[]{:T(128)S(6)} %add.164, s32[]{:T(128)S(6)} %select_n.88), kind=kOutput, calls=%fused_computation.12.clone.1 | convolution fusion | flops 1369767936 | bytes 22517768 | tf_op jit(solution)/shard_map/while/body/eval_jaxpr/hqk,ka->qha/dot_general | solution.py:57
  182.3 0.9 copy-done.7
  183.2 8.8 %convolution_convert_fusion = bf16[384,4096]{1,0:T(8,128)(2,1)} fusion(bf16[384,1024]{0,1:T(8,128)(2,1)} %bitcast.69, bf16[1024,4096]{1,0:T(8,128)(2,1)} %param.16), kind=kOutput, calls=%fused_computation.26 | convolution fusion | flops 3222798336 | bytes 12320768 | tf_op jit(solution)/shard_map/dot_general | solution.py:12
  192.1 23.1 %reduce-scatter.2.cloned.1.call-done = bf16[384,2048]{1,0:T(8,128)(2,1)} async-done(((bf16[384,4096]{1,0:T(8,128)(2,1)}), bf16[384,2048]{1,0:T(8,128)(2,1)}) %reduce-scatter.2.cloned.1.call-update) | async-done | bytes 1572880 | tf_op jit(solution)/shard_map/reduce_scatter | solution.py:64
  215.1 2.0 add_convert_fusion
  217.8 2.2 all_gather.6
  221.0 79.4 %all-gather.2.cloned.1.call-done = bf16[1024,4096]{1,0:T(8,128)(2,1)} async-done(((bf16[16,4096]{1,0:T(8,128)(2,1)}), bf16[1024,4096]{1,0:T(8,128)(2,1)}) %all-gather.2.cloned.1.call-update) | async-done | bytes 8388624 | tf_op jit(solution)/shard_map/all_gather | solution.py:73
  300.4 10.5 %fusion.22 = (f32[1024]{0:T(1024)S(1)}, f32[1024,512]{0,1:T(8,128)}) fusion(bf16[1024,4096]{1,0:T(8,128)(2,1)} %all-gather.2.cloned.1.call-done, bf16[512,4096]{1,0:T(8,128)(2,1)} %param.19), kind=kOutput, calls=%fused_computation.46 | convolution fusion | flops 4295490560 | bytes 14684160 | tf_op jit(solution)/shard_map/dot_general | solution.py:72
  310.9 64.7 %pmax.7 = f32[1024]{0:T(1024)S(1)} all-reduce(f32[1024]{0:T(1024)S(1)} %get-tuple-element.149), channel_id=1, replica_groups=mesh['dp'=4,'seq'=16,'mp'=2] {'dp','seq','mp'}, use_global_device_ids=true, to_apply=%region_9.10 | all-reduce | flops 1024 | bytes 8192 | tf_op jit(solution)/shard_map/pmax | solution.py:86
  375.6 2.1 select_reduce_fusion
  377.7 64.3 %all-reduce.3 = (f32[1024]{0:T(1024)S(1)}, f32[1024]{0:T(1024)S(1)}) all-reduce(f32[1024]{0:T(1024)S(1)} %get-tuple-element.128, f32[1024]{0:T(1024)S(1)} %get-tuple-element.127), channel_id=4, replica_groups=mesh['dp'=4,'seq'=16,'mp'=2] {'dp','seq','mp'}, use_global_device_ids=true, to_apply=%region_11.12.clone | all-reduce | flops 2048 | bytes 16384
  (48 shorter events, 4.3 us)
Async XLA Ops:
  11.6 107.2 %all-to-all-start = ((bf16[16,2,384,256]{3,2,1,0:T(8,128)(2,1)}), bf16[16,2,384,256]{3,2,1,0:T(8,128)(2,1)}, u32[]{:S(2)}, u32[]{:S(2)}) async-start(bf16[16,2,384,256]{3,2,1,0:T(8,128)(2,1)} %stack.11), calls=%async_computation | async-start | bytes 12582912 | tf_op jit(solution)/shard_map/all_to_all | solution.py:30
  20.2 194.9 %reduce-scatter.2.cloned.1.call-start = ((), (), s32[]{:S(2)}) async-start(), calls=%async_computation.2 | async-start | bytes 4718592 | tf_op jit(solution)/shard_map/reduce_scatter | solution.py:64
  122.0 4.2 copy-start
  122.0 4.2 copy-start.3
  144.7 9.0 %copy-start.6 = (bf16[2,384,512]{1,2,0:T(8,128)(2,1)S(1)}, bf16[2,384,512]{1,2,0:T(8,128)(2,1)}, u32[]{:S(2)}) copy-start(bf16[2,384,512]{1,2,0:T(8,128)(2,1)} %get-tuple-element.223) | copy-start | bytes 2359300 | tf_op jit(solution)/shard_map/while
  153.8 0.9 copy-start.7
  173.2 9.0 %copy-start.6 = (bf16[2,384,512]{1,2,0:T(8,128)(2,1)S(1)}, bf16[2,384,512]{1,2,0:T(8,128)(2,1)}, u32[]{:S(2)}) copy-start(bf16[2,384,512]{1,2,0:T(8,128)(2,1)} %get-tuple-element.223) | copy-start | bytes 2359300 | tf_op jit(solution)/shard_map/while
  182.3 0.9 copy-start.7
  183.2 8.9 %copy-start.8 = (s32[16]{0:T(128)S(1)}, s32[16]{0:T(128)}, u32[]{:S(2)}) copy-start(s32[16]{0:T(128)} %param.20) | copy-start | bytes 196
  192.0 23.2 %copy-start.2 = (bf16[384,2048]{1,0:T(8,128)(2,1)S(1)}, bf16[384,2048]{1,0:T(8,128)(2,1)}, u32[]{:S(2)}) copy-start(bf16[384,2048]{1,0:T(8,128)(2,1)} %param.17) | copy-start | bytes 4718596
  192.0 28.2 %copy-start.4 = (f32[4096]{0:T(1024)S(1)}, f32[4096]{0:T(1024)}, u32[]{:S(2)}) copy-start(f32[4096]{0:T(1024)} %param.18) | copy-start | bytes 49156
  192.0 108.4 %all-gather.2.cloned.1.call-start = ((), (), s32[]{:S(2)}) async-start(), calls=%async_computation.3 | async-start | bytes 8519680 | tf_op jit(solution)/shard_map/all_gather | solution.py:73
  217.2 93.7 %copy-start.1 = (bf16[384,2048]{1,0:T(8,128)(2,1)}, bf16[384,2048]{1,0:T(8,128)(2,1)S(1)}, u32[]{:S(2)}) copy-start(bf16[384,2048]{1,0:T(8,128)(2,1)S(1)} %add_convert_fusion) | copy-start | bytes 4718596
  221.0 154.5 %copy-start.5 = (s32[1024]{0:T(1024)S(1)}, s32[1024]{0:T(1024)}, u32[]{:S(2)}) copy-start(s32[1024]{0:T(1024)} %param.21) | copy-start | bytes 12292
Sparse Core Ops, SparseCore 0:
  192.1 22.9 reduce-scatter.1
  221.1 79.2 all-gather.1
